TPU v7x, 32 devices: a whole 2x2x4 slice. The times are simulated.
32 devices in a mesh: groups: 2 (over x), ctx: 16 (over z, y, core).
Axes of the slice: x: 2, y: 2, z: 4, core: 2. Of those that a mesh axis runs over, the one named last changes fastest.
Arguments:
- tokens: bfloat16 [4096, 2880], P(('groups', 'ctx')), parts along dimension 0, may hold values from -6 to 6
- lengths: int32 [8], P('groups'), parts along dimension 0, may hold values from 1 to 1536, 2048 in all
- attn_gain: float32 [2880], replicated, may hold values from 0.1 to 1.9
- w_query: bfloat16 [2880, 2048], P('ctx'), may hold values from -2 to 2
- w_key: bfloat16 [2880, 256], replicated, may hold values from -1 to 1
- w_value: bfloat16 [2880, 256], replicated, may hold values from -0.109375 to 0.109375
- sinks: float32 [32], replicated, may hold values from -2 to 4
- w_out: bfloat16 [2048, 2880], P('ctx'), may hold values from -0.5 to 0.5
- moe_gain: float32 [2880], replicated, may hold values from 0.1 to 1.9
- routes: int32 [4096, 4], P(('groups', 'ctx')), parts along dimension 0, may hold values from 0 to 7, all different within a row; in each aligned block of 128 rows (0 to 127, 128 to 255, ...) at most 68 rows name the same one
- route_weights: float32 [4096, 4], P(('groups', 'ctx')), parts along dimension 0, may hold values from 0.05 to 1
- w_gate: bfloat16 [16, 2880, 768], P('ctx'), may hold values from -0.109375 to 0.109375
- w_up: bfloat16 [16, 2880, 768], P('ctx'), may hold values from -0.109375 to 0.109375
- w_down: bfloat16 [16, 768, 2880], P('ctx'), may hold values from -0.15625 to 0.15625
Outputs:
- result: bfloat16 [4096, 2880], P(('groups', 'ctx')), parts along dimension 0
There are 2 independent parts, one for each index of `groups`. A program takes and returns all parts, laid end to end along the dimension named above; an argument that names none is the same for every part. Nothing has to cross between parts.
Inputs may be any that keep to these rules, and one draw needn't show every extreme that they name: lengths of the 4 requests packed in order into the 2048 tokens; they sum to 2048. `routes`: each token names 4 different experts; among the 128 tokens of one index of ctx no expert is named by more than 68 tokens, a bound that some block reaches.
All inputs are finite; a program needn't handle non-finite values.
Results may differ from a plain program's by a relative error of at most 0.014.
Values may be sent and summed in bfloat16 or wider, within the bound.
A program may use at most 128 MiB of HBM per device.

v0:
```python
import jax
import jax.numpy as jnp
from jax import lax
from jax.sharding import PartitionSpec as P

HD = 64
SPLITS = 2
TOP = 4


EPS = 1e-05
THETA = 150000.0
ALPHA = 1.702
SCALE = 0.125
NEGATIVE = -1e30


def from_partner(x, axis, stride):
    return lax.ppermute(x, axis, [(i, i ^ 1 << stride) for i in range(lax.axis_size(axis))])


def rms_scale(values, gain_vec):
    wide = values.astype(jnp.float32)
    inverse = lax.rsqrt(jnp.mean(wide * wide, axis=-1, keepdims=True) + EPS)
    return (wide * inverse * gain_vec).astype(jnp.bfloat16)


def rotate(values, positions):
    half_size = values.shape[-1] // 2
    freqs = THETA ** (-jnp.arange(half_size, dtype=jnp.float32) / half_size)
    angles = positions.astype(jnp.float32)[:, None] * freqs[None, :]
    cosine = jnp.cos(angles)[:, None, :]
    sine = jnp.sin(angles)[:, None, :]
    first = values[..., :half_size]
    second = values[..., half_size:]
    return jnp.concatenate(
        [first * cosine - second * sine, second * cosine + first * sine], axis=-1
    )


def segment_of(positions, doc_ends):
    return jnp.sum((positions[:, None] >= doc_ends[None, :]).astype(jnp.int32), axis=1)


def expert_rows(inputs, gate_mat, up_mat, down_mat):
    gate_val = jnp.dot(inputs, gate_mat, preferred_element_type=jnp.float32)
    up_val = jnp.dot(inputs, up_mat, preferred_element_type=jnp.float32)
    hidden = ((up_val + 1.0) * gate_val * jax.nn.sigmoid(ALPHA * gate_val)).astype(jnp.bfloat16)
    return jnp.dot(hidden, down_mat, preferred_element_type=jnp.float32).astype(jnp.bfloat16)


def per_device(
    tokens,
    lengths,
    attn_gain,
    w_query,
    w_key,
    w_value,
    sinks,
    w_out,
    moe_gain,
    routes,
    route_weights,
    w_gate,
    w_up,
    w_down,
):
    tok_rows, model_width = tokens.shape
    devices = lax.axis_size("ctx")
    my_rank = lax.axis_index("ctx")
    num_heads = w_query.shape[1] // HD
    kv_heads = w_key.shape[1] // HD
    group_size = num_heads // kv_heads
    doc_ends = jnp.cumsum(lengths)
    positions = my_rank * tok_rows + jnp.arange(tok_rows, dtype=jnp.int32)
    normed = rms_scale(tokens, attn_gain)
    cols_part = normed
    raw_query = jnp.dot(
        cols_part,
        lax.all_gather(w_query, "ctx", axis=0, tiled=True),
        preferred_element_type=jnp.float32,
    )
    raw_key = jnp.dot(normed, w_key, preferred_element_type=jnp.float32)
    val_flat = jnp.dot(normed, w_value, preferred_element_type=jnp.float32).astype(jnp.bfloat16)
    queries = rotate(raw_query.reshape(tok_rows, num_heads, HD), positions).astype(jnp.bfloat16)
    key_rot = rotate(raw_key.reshape(tok_rows, kv_heads, HD), positions).astype(jnp.bfloat16)
    local_segment = segment_of(positions, doc_ends)
    grouped = queries.reshape(tok_rows, kv_heads, group_size, HD)

    def attend_block(state_now, key_part, val_part, key_pos):
        run_max, run_sum, run_acc = state_now
        allowed = (local_segment[:, None] == segment_of(key_pos, doc_ends)[None, :]) & (
            key_pos[None, :] <= positions[:, None]
        )
        scores = (
            jnp.einsum("tkgd,skd->tkgs", grouped, key_part, preferred_element_type=jnp.float32)
            * SCALE
        )
        scores = jnp.where(allowed[:, None, None, :], scores, NEGATIVE)
        new_max = jnp.maximum(run_max, jnp.max(scores, axis=-1))
        rescale = jnp.exp(run_max - new_max)
        weights = jnp.exp(scores - new_max[..., None])
        new_sum = run_sum * rescale + jnp.sum(weights, axis=-1)
        new_acc = run_acc * rescale[..., None] + jnp.einsum(
            "tkgs,skd->tkgd",
            weights.astype(jnp.bfloat16),
            val_part,
            preferred_element_type=jnp.float32,
        )
        return (new_max, new_sum, new_acc)

    sink_grid = jnp.broadcast_to(
        sinks.reshape(kv_heads, group_size)[None], (tok_rows, kv_heads, group_size)
    )
    initial = (
        sink_grid,
        jnp.ones((tok_rows, kv_heads, group_size), jnp.float32),
        jnp.zeros((tok_rows, kv_heads, group_size, HD), jnp.float32),
    )
    key_flat = key_rot.reshape(tok_rows, kv_heads * HD)
    key_part = lax.all_gather(key_flat, "ctx", axis=0, tiled=True).reshape(-1, kv_heads, HD)
    val_part = lax.all_gather(val_flat, "ctx", axis=0, tiled=True).reshape(-1, kv_heads, HD)
    key_count = key_part.shape[0]
    key_pos = jnp.arange(key_count, dtype=jnp.int32)

    def scan_step(inner_state, block_index):
        block_start = block_index * 512
        updated = attend_block(
            inner_state,
            lax.dynamic_slice_in_dim(key_part, block_start, 512, 0),
            lax.dynamic_slice_in_dim(val_part, block_start, 512, 0),
            lax.dynamic_slice_in_dim(key_pos, block_start, 512, 0),
        )
        return (updated, None)

    final_state, unused = lax.scan(scan_step, initial, jnp.arange(key_count // 512))
    run_max, run_sum, run_acc = final_state
    attended = (run_acc / run_sum[..., None]).astype(jnp.bfloat16).reshape(tok_rows, num_heads * HD)
    cols_part = attended
    projected = jnp.dot(
        cols_part,
        lax.all_gather(w_out, "ctx", axis=0, tiled=True),
        preferred_element_type=jnp.float32,
    )
    mixed = (tokens.astype(jnp.float32) + projected).astype(jnp.bfloat16)
    expert_in = rms_scale(mixed, moe_gain)
    experts_num = devices // SPLITS
    capacity = tok_rows * TOP * 17 // (16 * experts_num)
    half_cap = capacity // 2
    flat_routes = routes.reshape(-1)
    onehot = (flat_routes[:, None] == jnp.arange(experts_num, dtype=jnp.int32)[None, :]).astype(
        jnp.int32
    )
    slots = jnp.sum((jnp.cumsum(onehot, axis=0) - 1) * onehot, axis=1)
    targets = flat_routes * capacity + slots
    select = jnp.sum(
        (
            jnp.arange(experts_num * capacity, dtype=jnp.int32)[:, None, None]
            == targets.reshape(tok_rows, TOP)[None]
        ).astype(jnp.int32),
        axis=2,
    ).astype(jnp.bfloat16)
    packed = (
        jnp.dot(select, expert_in, preferred_element_type=jnp.float32)
        .astype(jnp.bfloat16)
        .reshape(experts_num, capacity, model_width)
    )
    lower_first = my_rank % 2 == 0
    halves = packed.reshape(devices, half_cap, model_width)
    own_half = lax.all_to_all(halves, "ctx", split_axis=0, concat_axis=0, tiled=True)
    mate_half = from_partner(own_half, "ctx", 0)
    ordered = jnp.where(
        lower_first,
        jnp.concatenate([own_half, mate_half], axis=1),
        jnp.concatenate([mate_half, own_half], axis=1),
    )
    partial_value = expert_rows(
        ordered.reshape(-1, model_width), w_gate[0], w_up[0], w_down[0]
    ).reshape(ordered.shape)
    first_rows = partial_value[:, :half_cap]
    second_rows = partial_value[:, half_cap:]
    kept = jnp.where(lower_first, first_rows, second_rows)
    given = jnp.where(lower_first, second_rows, first_rows)
    received = from_partner(given, "ctx", 0)
    pair_sum = (kept.astype(jnp.float32) + received.astype(jnp.float32)).astype(jnp.bfloat16)
    returned = lax.all_to_all(pair_sum, "ctx", split_axis=0, concat_axis=0, tiled=True)
    summed = returned.reshape(experts_num, capacity, model_width)
    summed = (
        lax.optimization_barrier(summed)
        .astype(jnp.float32)
        .reshape(experts_num * capacity, model_width)
    )
    picked = jnp.take(summed, targets, axis=0).reshape(tok_rows, TOP, model_width)
    expert_sum = jnp.sum(picked * route_weights[..., None], axis=1)
    return (mixed.astype(jnp.float32) + expert_sum).astype(jnp.bfloat16)


def solution(mesh):
    placed = (
        P(("groups", "ctx"), None),
        P("groups"),
        P(),
        P("ctx", None),
        P(),
        P(),
        P(),
        P("ctx", None),
        P(),
        P(("groups", "ctx"), None),
        P(("groups", "ctx"), None),
        P("ctx", None, None),
        P("ctx", None, None),
        P("ctx", None, None),
    )
    return jax.shard_map(
        per_device,
        mesh=mesh,
        in_specs=placed,
        out_specs=P(("groups", "ctx"), None),
        check_vma=False,
    )
```

profile of v0, /device:TPU:15, one launch (start us, length us, event | category | flops | bytes accessed | tf_op | source)
XLA Modules:
  0.0 604.6 jit_solution(7229030767309414924)
XLA Ops:
  18.1 30.9 %all-gather.8.cloned.1.call-done = bf16[2048,256]{1,0:T(8,128)(2,1)} async-done(((bf16[128,256]{1,0:T(8,128)(2,1)}), bf16[2048,256]{1,0:T(8,128)(2,1)}) %all-gather.8.cloned.1.call-update) | async-done | bytes 1048592 | tf_op jit(solution)/shard_map/all_gather | solution.py:122
  51.3 95.7 %all-gather.12.cloned.1.call-done = bf16[16,180,2048]{2,1,0:T(8,128)(2,1)} async-done(((bf16[1,180,2048]{2,1,0:T(8,128)(2,1)}), bf16[16,180,2048]{2,1,0:T(8,128)(2,1)}) %all-gather.12.cloned.1.call-update) | async-done | bytes 11796496 | tf_op jit(solution)/shard_map/all_gather | solution.py:80
  147.0 11.6 %reshape.303 = bf16[2880,2048]{1,0:T(8,128)(2,1)} reshape(bf16[16,180,2048]{2,1,0:T(8,128)(2,1)} %all-gather.12.cloned.1.call-done) | data formatting | bytes 23592960
  158.6 8.3 %fusion.65 = f32[128,2048]{0,1:T(8,128)S(1)} fusion(bf16[2880,2048]{1,0:T(8,128)(2,1)} %reshape.303, bf16[128,2880]{0,1:T(8,128)(2,1)S(1)} %copy-done.7, f32[2880]{0:T(1024)S(1)} %copy-done.10, f32[128]{0:T(128)S(1)} %copy-done.14), kind=kOutput, calls=%fused_computation.95 | convolution fusion | flops 1511424000 | bytes 13594368 | tf_op jit(solution)/shard_map/dot_general | solution.py:78
  167.1 19.0 %all-gather.6.cloned.1.call-done = bf16[2048,256]{0,1:T(8,128)(2,1)} async-done(((bf16[128,256]{0,1:T(8,128)(2,1)}), bf16[2048,256]{0,1:T(8,128)(2,1)}) %all-gather.6.cloned.1.call-update) | async-done | bytes 1048592 | tf_op jit(solution)/shard_map/all_gather | solution.py:121
  186.2 58.9 %while.15 = (s32[]{:T(128)}, f32[128,4,8]{0,2,1:T(8,128)S(1)}, f32[128,4,8]{0,2,1:T(8,128)S(1)}, f32[128,4,8,64]{0,3,2,1:T(8,128)S(1)}, s32[128]{0:T(128)S(1)}, ...) while((s32[]{:T(128)}, f32[128,4,8]{0,2,1:T(8,128)S(1)}, ...), condition=%wide.region_7.8_spmd.clone, body=%wide.region_3.7_spmd.clone.sunk | while | flops 560940672 | bytes 62404372 | solution.py:136
  190.1 3.2 copy-done.2
  195.1 6.0 fusion.91
  205.1 3.2 copy-done.2
  210.2 5.6 fusion.91
  224.7 5.6 fusion.91
  239.3 5.8 fusion.91
  246.1 37.4 %all-gather.10.cloned.1.call-done = bf16[2048,2880]{0,1:T(8,128)(2,1)} async-done(((bf16[128,2880]{0,1:T(8,128)(2,1)}), bf16[2048,2880]{0,1:T(8,128)(2,1)}) %all-gather.10.cloned.1.call-update) | async-done | bytes 11796496 | tf_op jit(solution)/shard_map/all_gather | solution.py:142
  283.4 6.3 %multiply_reduce_fusion.1 = (f32[128]{0:T(128)S(1)}, f32[128,2880]{0,1:T(8,128)S(1)}) fusion(bf16[2048,2880]{0,1:T(8,128)(2,1)} %all-gather.10.cloned.1.call-done, bf16[128,2048]{0,1:T(8,128)(2,1)} %bitcast.98, bf16[128,2880]{0,1:T(8,128)(2,1)S(1)} %copy-done.7), kind=kOutput, calls=%fused_computation.59 | convolution fusion | flops 1512161152 | bytes 14533120 | tf_op jit(solution)/shard_map/dot_general | solution.py:140
  292.6 4.7 reshape_reshape.3
  297.3 90.1 %all_to_all.10 = bf16[16,34,2880]{2,1,0:T(8,128)(2,1)S(1)} all-to-all(bf16[16,34,2880]{2,1,0:T(8,128)(2,1)} %reshape_reshape.3), channel_id=1, replica_groups=mesh['groups'=2,'ctx'=16] {'ctx'}, dimensions={0} | all-to-all | bytes 6266880 | tf_op jit(solution)/shard_map/all_to_all | solution.py:170
  391.7 5.7 collective-permute-done
  399.9 5.0 maximum_select_fusion
  404.9 9.0 %select_n.77 = bf16[1088,2880]{1,0:T(8,128)(2,1)} reshape(bf16[16,68,2880]{2,1,0:T(8,128)(2,1)} %maximum_select_fusion) | data formatting | bytes 12533760 | tf_op jit(solution)/shard_map/jit(_where)/select_n | solution.py:172
  413.8 9.9 %fusion.25 = f32[1088,768]{1,0:T(8,128)} fusion(bf16[1088,2880]{1,0:T(8,128)(2,1)} %select_n.77, bf16[1,2880,768]{2,1,0:T(8,128)(2,1)} %param.27), kind=kOutput, calls=%fused_computation.33 | convolution fusion | flops 4812963840 | bytes 14032896 | tf_op jit(solution)/shard_map/dot_general | solution.py:46
  423.8 20.3 %convolution_convert_fusion = bf16[1088,2880]{1,0:T(8,128)(2,1)} fusion(bf16[1,768,2880]{1,2,0:T(8,128)(2,1)} %param.29, f32[1088,768]{1,0:T(8,128)} %fusion.25, bf16[1088,2880]{1,0:T(8,128)(2,1)} %select_n.77, bf16[1,2880,768]{2,1,0:T(8,128)(2,1)} %param.28), kind=kOutput, calls=%fused_computation.27 | convolution fusion | flops 9635745792 | bytes 24723456 | tf_op jit(solution)/shard_map/dot_general | solution.py:49
  444.1 8.4 %reshape.288 = bf16[16,68,2880]{2,1,0:T(8,128)(2,1)} reshape(bf16[1088,2880]{1,0:T(8,128)(2,1)} %convolution_convert_fusion) | data formatting | bytes 12533760 | tf_op jit(solution)/shard_map/reshape | solution.py:179
  452.5 4.4 broadcast_select_fusion
  457.7 5.4 collective-permute-done.1
  463.0 3.8 add_convert_fusion
  466.9 7.0 %all-to-all-start.1 = ((bf16[16,34,2880]{2,1,0:T(8,128)(2,1)}), bf16[16,34,2880]{2,1,0:T(8,128)(2,1)}, u32[]{:S(2)}, u32[]{:S(2)}) async-start(bf16[16,34,2880]{2,1,0:T(8,128)(2,1)} %add_convert_fusion), calls=%async_computation.1 | async-start | bytes 7536640 | tf_op jit(solution)/shard_map/all_to_all | solution.py:186
  474.3 82.7 %all-to-all-done.1 = bf16[16,34,2880]{2,1,0:T(8,128)(2,1)} async-done(((bf16[16,34,2880]{2,1,0:T(8,128)(2,1)}), bf16[16,34,2880]{2,1,0:T(8,128)(2,1)}, u32[]{:S(2)}, u32[]{:S(2)}) %all-to-all-start.1) | async-done | bytes 3133472 | tf_op jit(solution)/shard_map/all_to_all | solution.py:186
  557.0 5.0 reshape.289
  562.1 5.4 reshape.293
  567.5 9.7 %gather_fusion = f32[512,2880]{1,0:T(8,128)} fusion(f32[544,2880]{1,0:T(8,128)} %reshape.293, s32[1024]{0:T(1024)S(1)} %pad_clamp_fusion), kind=kCustom, calls=%fused_computation | custom fusion | bytes 11798528 | tf_op jit(solution)/shard_map/jit(_take)/gather | solution.py:193
  577.2 7.6 %gather.7 = f32[128,4,2880]{2,1,0:T(4,128)} reshape(f32[512,2880]{1,0:T(8,128)} %gather_fusion) | data formatting | bytes 11796480 | tf_op jit(solution)/shard_map/jit(_take)/gather | solution.py:193
  584.9 8.3 %multiply_reduce_fusion = f32[128,2880]{1,0:T(8,128)S(1)} fusion(f32[128,4,2880]{2,1,0:T(4,128)} %gather.7, f32[128,4]{1,0:T(8,128)S(1)} %copy.74, pred[128,4]{1,0:T(8,128)(4,1)S(1)} %copy.67), kind=kLoop, calls=%fused_computation.30 | loop fusion | flops 4055040 | bytes 7375360 | tf_op jit(solution)/shard_map/reduce_sum | solution.py:194
  (137 shorter events, 56.7 us)
Async XLA Ops:
  6.5 1.7 copy-start
  6.5 5.3 copy-start.7
  6.5 5.3 copy-start.9
  6.5 42.5 %all-gather.8.cloned.1.call-start = ((), (), s32[]{:S(2)}) async-start(), calls=%async_computation.3 | async-start | bytes 1114112 | tf_op jit(solution)/shard_map/all_gather | solution.py:122
  8.2 7.4 %copy-start.8 = (s32[128,4]{0,1:T(4,128)S(1)}, s32[128,4]{0,1:T(4,128)}, u32[]{:S(2)}) copy-start(s32[128,4]{0,1:T(4,128)} %param.25) | copy-start | bytes 6148
  8.2 7.7 %copy-start.16 = (s32[4]{0:T(128)S(1)}, s32[4]{0:T(128)}, u32[]{:S(2)}) copy-start(s32[4]{0:T(128)} %param.17) | copy-start | bytes 52
  8.2 7.9 %copy-start.15 = (f32[32]{0:T(128)S(1)}, f32[32]{0:T(128)}, u32[]{:S(2)}) copy-start(f32[32]{0:T(128)} %param.22) | copy-start | bytes 388
  8.3 9.6 %copy-start.13 = (f32[128]{0:T(128)}, f32[128]{0:T(128)S(1)}, u32[]{:S(2)}) copy-start(f32[128]{0:T(128)S(1)} %add_rsqrt_fusion.1) | copy-start | bytes 1540
  10.9 136.1 %all-gather.12.cloned.1.call-start = ((), (), s32[]{:S(2)}) async-start(), calls=%async_computation.5 | async-start | bytes 12812288 | tf_op jit(solution)/shard_map/all_gather | solution.py:80
  11.6 174.5 %all-gather.6.cloned.1.call-start = ((), (), s32[]{:S(2)}) async-start(), calls=%async_computation.2 | async-start | bytes 1114112 | tf_op jit(solution)/shard_map/all_gather | solution.py:121
  15.0 268.4 %all-gather.10.cloned.1.call-start = ((), (), s32[]{:S(2)}) async-start(), calls=%async_computation.4 | async-start | bytes 12533760 | tf_op jit(solution)/shard_map/all_gather | solution.py:142
  51.3 107.3 %copy-start.10 = (f32[2880]{0:T(1024)S(1)}, f32[2880]{0:T(1024)}, u32[]{:S(2)}) copy-start(f32[2880]{0:T(1024)} %param.18) | copy-start | bytes 34564
  51.3 107.3 %copy-start.14 = (f32[128]{0:T(128)S(1)}, f32[128]{0:T(128)}, u32[]{:S(2)}) copy-start(f32[128]{0:T(128)} %copy-done.13) | copy-start | bytes 1540
  190.1 3.2 copy-start.2
  205.1 3.2 copy-start.2
  219.7 3.2 copy-start.2
  234.3 3.2 copy-start.2
  283.4 6.3 %copy-start.11 = (f32[2880]{0:T(1024)S(1)}, f32[2880]{0:T(1024)}, u32[]{:S(2)}) copy-start(f32[2880]{0:T(1024)} %param.24) | copy-start | bytes 34564
  289.7 7.6 %copy-start.6 = (f32[128,2880]{0,1:T(8,128)}, f32[128,2880]{0,1:T(8,128)S(1)}, u32[]{:S(2)}) copy-start(f32[128,2880]{0,1:T(8,128)S(1)} %get-tuple-element.161) | copy-start | bytes 4423684
  387.4 1.8 copy-start.4
  391.3 6.1 %collective-permute-start = (bf16[16,34,2880]{2,0,1:T(8,128)(2,1)}, bf16[16,34,2880]{2,0,1:T(8,128)(2,1)}, u32[]{:S(2)}, u32[]{:S(2)}) collective-permute-start(bf16[16,34,2880]{2,0,1:T(8,128)(2,1)} %copy.68), channel_id=1, source_target_pairs={{0,1},{1,0},{2,3},{3,2},{4,5},{5,4},{6,7},{7,6},{8,9},{9,8},{10,11... | collective-permute-start | bytes 9400328 | tf_op jit(solution)/shard_map/ppermute | solution.py:19
  391.6 8.2 %copy-start.5 = (bf16[16,34,2880]{2,1,0:T(8,128)(2,1)S(1)}, bf16[16,34,2880]{2,1,0:T(8,128)(2,1)}, u32[]{:S(2)}) copy-start(bf16[16,34,2880]{2,1,0:T(8,128)(2,1)} %copy-done.4) | copy-start | bytes 9400324
  456.9 6.2 %copy-start.3 = (bf16[16,68,2880]{2,1,0:T(8,128)(2,1)S(1)}, bf16[16,68,2880]{2,1,0:T(8,128)(2,1)}, u32[]{:S(2)}) copy-start(bf16[16,68,2880]{2,1,0:T(8,128)(2,1)} %reshape.288) | copy-start | bytes 18800644
  457.2 5.8 collective-permute-start.1
  466.9 7.3 %copy-start.12 = (f32[128,4]{0,1:T(4,128)S(1)}, f32[128,4]{0,1:T(4,128)}, u32[]{:S(2)}) copy-start(f32[128,4]{0,1:T(4,128)} %param.26) | copy-start | bytes 6148
  466.9 90.2 %all-to-all-start.1 = ((bf16[16,34,2880]{2,1,0:T(8,128)(2,1)}), bf16[16,34,2880]{2,1,0:T(8,128)(2,1)}, u32[]{:S(2)}, u32[]{:S(2)}) async-start(bf16[16,34,2880]{2,1,0:T(8,128)(2,1)} %add_convert_fusion), calls=%async_computation.1 | async-start | bytes 7536640 | tf_op jit(solution)/shard_map/all_to_all | solution.py:186
  584.9 12.7 %copy-start.1 = (bf16[2880,256]{1,0:T(8,128)(2,1)S(1)}, bf16[2880,256]{1,0:T(8,128)(2,1)}, u32[]{:S(2)}) copy-start(bf16[2880,256]{1,0:T(8,128)(2,1)} %param.21) | copy-start | bytes 4423684
Sparse Core Ops, SparseCore 0:
  11.0 37.9 all-gather.7
  51.3 95.6 all-gather.11
  149.2 36.8 all-gather.5
  188.1 95.2 all-gather.9
where the time goes:
time: 608 us; the launch traced here: 605 us
  waiting for transfers between devices  278 us (46%)
  blocking collectives  90.1 us (15%)
  local copies, waits for them, and re-layouts  89 us (15%)
  matrix products  84.7 us (14%)
  other arithmetic  38 us (6%)
  between operations  13.9 us (2%)
  starting transfers between devices  8.08 us (1%)
    all_gather x1, waiting for transfers between devices, per_device(): lax.all_gather(w_query, 'ctx', axis=0, tiled=True)  95.7 us
    all_to_all x1, blocking collectives, per_device(): lax.all_to_all(halves, 'ctx', split_axis=0, concat_axis=0, tiled=True)  90.1 us
    all_to_all x1, waiting for transfers between devices, per_device(): lax.all_to_all(pair_sum, 'ctx', split_axis=0, concat_axis=0, tiled=True)  82.7 us
    all_gather x1, waiting for transfers between devices, per_device(): lax.all_gather(w_out, 'ctx', axis=0, tiled=True)  37.4 us
    all_gather x1, waiting for transfers between devices, per_device(): lax.all_gather(val_flat, 'ctx', axis=0, tiled=True)  30.9 us
    dot_general x4, matrix products, attend_block(): jnp.einsum('tkgs,skd->tkgd', weights.astype(jnp.bfloat16), val_part, pref...  23 us
    dot_general x1, matrix products, expert_rows(): jnp.dot(hidden, down_mat, preferred_element_type=jnp.float32)  20.3 us
    all_gather x1, waiting for transfers between devices, per_device(): lax.all_gather(key_flat, 'ctx', axis=0, tiled=True)  19 us
  transfers between devices with their start and end apart: 7, of which 7 were waited for; matrix products, arithmetic and copies ran while one was open for 12% of the time, Pallas kernels for 0%

commit v1 on v0

v1 whole, which is shorter than its diff:
```python
import functools

import jax
import jax.numpy as jnp
from jax import lax
from jax.experimental import pallas as pl
from jax.experimental.pallas import tpu as pltpu
from jax.sharding import PartitionSpec as P

HD = 64
EPS = 1e-05
THETA = 150000.0
ALPHA = 1.702
SCALE = 0.125
NEGATIVE = -1e30
MESH = pl.DeviceIdType.MESH
VMEM = pl.BlockSpec(memory_space=pltpu.VMEM)
LIMIT = 63 * 1024 * 1024


def rms_scale(values, gain_vec):
    wide = values.astype(jnp.float32)
    inverse = lax.rsqrt(jnp.mean(wide * wide, axis=-1, keepdims=True) + EPS)
    return (wide * inverse * gain_vec).astype(jnp.bfloat16)


class Ring:
    def __init__(self, chips):
        self.chips = chips
        self.me = lax.axis_index("ctx")
        self.core = lax.rem(self.me, 2)
        chip = self.me // 2
        self.fold = chips == 8
        if self.fold:
            z, y = chip // 2, lax.rem(chip, 2)
            self.pos = z + y * (chips - 1 - 2 * z)
        else:
            self.pos = chip
        self.way = 1 - 2 * self.core
        self.partner = self.me + self.way
        self.next = self.owner(-1)
        self.prev = self.owner(1)

    def index(self, pos, core):
        pos = lax.rem(pos + 2 * self.chips, self.chips)
        if self.fold:
            y = pos // (self.chips // 2)
            z = pos + y * (self.chips - 1 - 2 * pos)
            chip = z * 2 + y
        else:
            chip = pos
        return chip * 2 + core

    def owner(self, step):
        return self.index(self.pos - self.way * step, self.core)

    def partner_owner(self, step):
        return self.index(self.pos + self.way * step, 1 - self.core)

    def barrier(self):
        sem = pltpu.get_barrier_semaphore()
        for other in (self.next, self.prev, self.partner):
            pl.semaphore_signal(sem, inc=1, device_id={"ctx": other}, device_id_type=MESH)
        pl.semaphore_wait(sem, 3)


def gather_ring(ring, pieces, sems, work):
    ring_send, ring_recv, part_send, part_recv = sems
    chips = ring.chips

    def copies(i, step, own):
        source, slots, view = pieces[i]
        who = ring.owner(step)
        src = view(source) if own else view(slots.at[who])
        out = []
        for target, send, recv in (
            (ring.next, ring_send, ring_recv),
            (ring.partner, part_send, part_recv),
        ):
            at = step + 1 if target is ring.next else step
            out.append(
                pltpu.make_async_remote_copy(
                    src_ref=src,
                    dst_ref=view(slots.at[who]),
                    send_sem=send.at[i, step],
                    recv_sem=recv.at[i, at],
                    device_id={"ctx": target},
                    device_id_type=MESH,
                )
            )
        return out

    def arrived(i, step, recv, who):
        slots, view = pieces[i][1], pieces[i][2]
        ref = view(slots.at[who])
        pltpu.make_async_copy(ref, ref, recv.at[i, step]).wait()

    ring.barrier()
    for i in range(len(pieces)):
        for copy in copies(i, 0, True):
            copy.start()
    for source, slots, view in pieces:
        view(slots.at[ring.me])[...] = view(source)[...]
    work(ring.me)

    def step(s, carry):
        who = ring.owner(s)
        for i in range(len(pieces)):
            arrived(i, s, ring_recv, who)
            onward, across = copies(i, s, False)

            @pl.when(s < chips - 1)
            def _():
                onward.start()

            across.start()
        work(who)
        late = ring.partner_owner(s - 1)
        for i in range(len(pieces)):
            arrived(i, s - 1, part_recv, late)
        work(late)
        return carry

    lax.fori_loop(1, chips, step, 0)
    late = ring.partner_owner(chips - 1)
    for i in range(len(pieces)):
        arrived(i, chips - 1, part_recv, late)
    work(late)

    def drain(s, carry):
        for i in range(len(pieces)):
            onward, across = copies(i, s, False)

            @pl.when(s < chips - 1)
            def _():
                onward.wait_send()

            across.wait_send()
        return carry

    lax.fori_loop(0, chips, drain, 0)


def ring_sems(count, chips):
    return [pltpu.SemaphoreType.DMA((count, chips))] * 4


def whole(ref):
    return ref


def cols(start, size):
    return lambda ref: ref.at[:, pl.ds(start, size)]


def rows(start, size):
    return lambda ref: ref.at[pl.ds(start, size), :]


def query_kernel(chips, lhs, kv, meta, weight, out, kv_all, meta_all, slots, *sems):
    ring = Ring(chips)
    half = weight.shape[1] // 2
    pieces = [
        (kv, kv_all, whole),
        (meta, meta_all, whole),
        (weight, slots, cols(0, half)),
        (weight, slots, cols(half, half)),
    ]
    out[...] = jnp.zeros_like(out)

    def work(who):
        out[...] += jnp.dot(lhs[who], slots[who], preferred_element_type=jnp.float32)

    gather_ring(ring, pieces, sems, work)


def attend_kernel(
    chips, query, key, value, sinks, start, weight, tokens, out, slots, bias, attended, *sems
):
    ring = Ring(chips)
    blocks, tok_rows, width = attended.shape
    per_block = width // HD
    seq = key.shape[1]
    group = query.shape[0] // key.shape[0]
    half = weight.shape[0] // 2
    pieces = [(weight, slots, rows(0, half)), (weight, slots, rows(half, half))]
    key_pos = lax.broadcasted_iota(jnp.int32, (tok_rows, seq), 1)
    row_pos = lax.broadcasted_iota(jnp.int32, (tok_rows, seq), 0) + ring.me * tok_rows
    allowed = (key_pos <= row_pos) & (key_pos >= start[...])
    bias[...] = jnp.where(allowed, 0.0, NEGATIVE)

    def work(who):
        heads = []
        for j in range(per_block):
            head = who * per_block + j
            kv_head = head // group
            scores = (
                lax.dot_general(
                    query[head],
                    key[kv_head],
                    (((1,), (1,)), ((), ())),
                    preferred_element_type=jnp.float32,
                )
                + bias[...]
            )
            sink = sinks[head]
            top = jnp.maximum(jnp.max(scores, axis=1, keepdims=True), sink)
            weights = jnp.exp(scores - top)
            total = jnp.sum(weights, axis=1, keepdims=True) + jnp.exp(sink - top)
            mixed = jnp.dot(
                weights.astype(jnp.bfloat16), value[kv_head], preferred_element_type=jnp.float32
            )
            heads.append(mixed / total)
        joined = heads[0] if per_block == 1 else jnp.concatenate(heads, axis=1)
        attended[who] = joined.astype(jnp.bfloat16)

    gather_ring(ring, pieces, sems, work)
    out[...] = tokens[...].astype(jnp.float32)

    def project(d, carry):
        out[...] += jnp.dot(attended[d], slots[d], preferred_element_type=jnp.float32)
        return carry

    lax.fori_loop(0, blocks, project, 0)


def dispatch_kernel(chips, rows_in, select, out, slots, *sems):
    ring = Ring(chips)
    half = rows_in.shape[0] // 2
    pieces = [(rows_in, slots, rows(0, half)), (rows_in, slots, rows(half, half))]

    def work(who):
        out[who] = jnp.dot(select[who], slots[who], preferred_element_type=jnp.float32).astype(
            jnp.bfloat16
        )

    gather_ring(ring, pieces, sems, work)


def combine_kernel(
    chips, partial, select, weights, mixed, out, cross_out, cross_in, ring_out, ring_in,
    ring_send, ring_recv, part_send, part_recv,
):
    ring = Ring(chips)
    tok_rows = mixed.shape[0]
    half = tok_rows // 2
    ring.barrier()

    def share(who, h):
        at = pl.ds(h * half, half)
        spread = jnp.dot(select[who, at, :], partial[who], preferred_element_type=jnp.float32)
        return spread * weights[who, at, :]

    def crossing(s, h):
        at = pl.ds(h * half, half)
        return pltpu.make_async_remote_copy(
            src_ref=cross_out.at[s, at, :],
            dst_ref=cross_in.at[s, at, :],
            send_sem=part_send.at[h, s],
            recv_sem=part_recv.at[h, s],
            device_id={"ctx": ring.partner},
            device_id_type=MESH,
        )

    def onward(s, h):
        at = pl.ds(h * half, half)
        return pltpu.make_async_remote_copy(
            src_ref=ring_out.at[s, at, :],
            dst_ref=ring_in.at[s, at, :],
            send_sem=ring_send.at[h, s],
            recv_sem=ring_recv.at[h, s],
            device_id={"ctx": ring.next},
            device_id_type=MESH,
        )

    def give(s):
        who = ring.partner_owner(s + 1)
        for h in range(2):
            at = pl.ds(h * half, half)
            cross_out[s, at, :] = share(who, h).astype(jnp.bfloat16)
            crossing(s, h).start()

    def own(s, h):
        total = share(ring.owner(s + 1), h)
        crossing(s, h).wait_recv()
        return total + cross_in[s, pl.ds(h * half, half), :].astype(jnp.float32)

    give(0)
    for h in range(2):
        ring_out[0, pl.ds(h * half, half), :] = own(0, h).astype(jnp.bfloat16)
        onward(0, h).start()
    give(1)

    def step(s, carry):
        for h in range(2):
            at = pl.ds(h * half, half)
            total = own(s, h)
            onward(s - 1, h).wait_recv()
            total = total + ring_in[s - 1, at, :].astype(jnp.float32)
            ring_out[s, at, :] = total.astype(jnp.bfloat16)
            onward(s, h).start()
        give(s + 1)
        return carry

    lax.fori_loop(1, chips - 1, step, 0)
    last = chips - 1
    for h in range(2):
        at = pl.ds(h * half, half)
        total = own(last, h)
        onward(last - 1, h).wait_recv()
        total = total + ring_in[last - 1, at, :].astype(jnp.float32)
        out[at, :] = (mixed[at, :].astype(jnp.float32) + total).astype(jnp.bfloat16)

    def drain(s, carry):
        for h in range(2):
            crossing(s, h).wait_send()

            @pl.when(s < chips - 1)
            def _():
                onward(s, h).wait_send()

        return carry

    lax.fori_loop(0, chips, drain, 0)


def call(kernel, chips, out_shape, scratch, identity, *args, smem=()):
    single = not isinstance(out_shape, (list, tuple))
    return pl.pallas_call(
        functools.partial(kernel, chips),
        out_shape=out_shape,
        in_specs=[
            pl.BlockSpec(memory_space=pltpu.SMEM) if i in smem else VMEM for i in range(len(args))
        ],
        out_specs=VMEM if single else [VMEM] * len(out_shape),
        scratch_shapes=scratch,
        compiler_params=pltpu.CompilerParams(
            collective_id=identity, has_side_effects=True, vmem_limit_bytes=LIMIT
        ),
    )(*args)


def per_device(
    tokens, lengths, attn_gain, w_query, w_key, w_value, sinks, w_out, moe_gain, routes,
    route_weights, w_gate, w_up, w_down,
):
    bf16, f32 = jnp.bfloat16, jnp.float32
    tok_rows, width = tokens.shape
    devices = lax.axis_size("ctx")
    chips = devices // 2
    me = lax.axis_index("ctx")
    q_cols = w_query.shape[1]
    num_heads = q_cols // HD
    kv_cols = w_key.shape[1]
    kv_heads = kv_cols // HD
    experts = chips
    capacity = tok_rows * 4 * 17 // (16 * experts)
    padded = -(-capacity // 16) * 16

    member = routes[:, :, None] == jnp.arange(experts, dtype=jnp.int32)[None, None, :]
    named = jnp.any(member, axis=1)
    lower = jnp.tril(jnp.ones((tok_rows, tok_rows), bf16))
    slot = jnp.dot(lower, named.astype(bf16), preferred_element_type=f32) - 1.0
    slot = jnp.where(named, slot, -1.0)
    routed_weight = jnp.sum(jnp.where(member, route_weights[:, :, None], 0.0), axis=1)
    meta = jnp.concatenate([slot, routed_weight], axis=1).T

    positions = me * tok_rows + jnp.arange(tok_rows, dtype=jnp.int32)
    freqs = THETA ** (-jnp.arange(HD // 2, dtype=f32) / (HD // 2))
    angles = positions.astype(f32)[:, None] * freqs[None, :]
    cosine, sine = jnp.cos(angles)[:, None, :], jnp.sin(angles)[:, None, :]

    def rotate(values):
        first, second = values[..., : HD // 2], values[..., HD // 2 :]
        return jnp.concatenate(
            [first * cosine - second * sine, second * cosine + first * sine], axis=-1
        ).astype(bf16)

    normed = rms_scale(tokens, attn_gain)
    raw_key = jnp.dot(normed, w_key, preferred_element_type=f32)
    value = jnp.dot(normed, w_value, preferred_element_type=f32).astype(bf16)
    key = rotate(raw_key.reshape(tok_rows, kv_heads, HD)).reshape(tok_rows, kv_cols)
    kv = jnp.concatenate([key, value], axis=1)
    lhs = normed.reshape(tok_rows, devices, width // devices).transpose(1, 0, 2)
    raw_query, kv_all, meta_all = call(
        query_kernel,
        chips,
        [
            jax.ShapeDtypeStruct((tok_rows, q_cols), f32),
            jax.ShapeDtypeStruct((devices,) + kv.shape, bf16),
            jax.ShapeDtypeStruct((devices,) + meta.shape, f32),
        ],
        [pltpu.VMEM((devices,) + w_query.shape, bf16)] + ring_sems(4, chips),
        0,
        lhs, kv, meta, w_query,
    )
    query = rotate(raw_query.reshape(tok_rows, num_heads, HD)) * SCALE
    query = query.astype(bf16).transpose(1, 0, 2)
    halves = kv_all.reshape(devices * tok_rows, 2, kv_heads, HD).transpose(1, 2, 0, 3)
    doc_ends = jnp.cumsum(lengths)
    start = jnp.max(
        jnp.where(positions[:, None] >= doc_ends[None, :], doc_ends[None, :], 0), axis=1
    )[:, None]
    projected = call(
        attend_kernel,
        chips,
        jax.ShapeDtypeStruct((tok_rows, width), f32),
        [
            pltpu.VMEM((devices,) + w_out.shape, bf16),
            pltpu.VMEM((tok_rows, devices * tok_rows), f32),
            pltpu.VMEM((devices, tok_rows, w_out.shape[0]), bf16),
        ]
        + ring_sems(2, chips),
        1,
        query, halves[0], halves[1], sinks, start, w_out, tokens,
        smem=(3,),
    )
    mixed = projected.astype(bf16)
    expert_in = rms_scale(mixed, moe_gain)
    expert = me // 2
    slot_all = lax.dynamic_index_in_dim(meta_all, expert, 1, keepdims=False)
    weight_all = lax.dynamic_index_in_dim(meta_all, experts + expert, 1, keepdims=False)
    places = jnp.arange(padded, dtype=jnp.int32).astype(f32)
    select = (slot_all[:, None, :] == places[None, :, None]).astype(bf16)
    select_back = (slot_all[:, :, None] == places[None, None, :]).astype(bf16)
    packed = call(
        dispatch_kernel,
        chips,
        jax.ShapeDtypeStruct((devices, padded, width), bf16),
        [pltpu.VMEM((devices, tok_rows, width), bf16)] + ring_sems(2, chips),
        2,
        expert_in, select,
    ).reshape(devices * padded, width)
    gate_val = jnp.dot(packed, w_gate[0], preferred_element_type=f32)
    up_val = jnp.dot(packed, w_up[0], preferred_element_type=f32)
    hidden = ((up_val + 1.0) * gate_val * jax.nn.sigmoid(ALPHA * gate_val)).astype(bf16)
    partial = jnp.dot(hidden, w_down[0], preferred_element_type=f32).astype(bf16)
    return call(
        combine_kernel,
        chips,
        jax.ShapeDtypeStruct((tok_rows, width), bf16),
        [pltpu.VMEM((chips, tok_rows, width), bf16)] * 2
        + [pltpu.VMEM((chips - 1, tok_rows, width), bf16)] * 2
        + ring_sems(2, chips),
        3,
        partial.reshape(devices, padded, width), select_back, weight_all[:, :, None], mixed,
    )


def solution(mesh):
    placed = (
        P(("groups", "ctx"), None),
        P("groups"),
        P(),
        P("ctx", None),
        P(),
        P(),
        P(),
        P("ctx", None),
        P(),
        P(("groups", "ctx"), None),
        P(("groups", "ctx"), None),
        P("ctx", None, None),
        P("ctx", None, None),
        P("ctx", None, None),
    )
    return jax.shard_map(
        per_device,
        mesh=mesh,
        in_specs=placed,
        out_specs=P(("groups", "ctx"), None),
        check_vma=False,
    )
```

time: 608 us -> 372 us (0.61)
  Pallas kernels: 0 us -> 286 us
  waiting for transfers between devices: 278 us -> 0 us
  blocking collectives: 90.1 us -> 0 us
  local copies, waits for them, and re-layouts: 89 us -> 32.6 us
  matrix products: 84.7 us -> 36 us
  other arithmetic: 38 us -> 13.5 us
  between operations: 13.9 us -> 0.25 us
  starting transfers between devices: 8.08 us -> 0 us
    pallas_call x0 -> x4, Pallas kernels: none -> 286 us  [call(): pl.pallas_call(functools.partial(kernel, chips), out_shape=out_shape, in_...]
    all_gather x4 -> x0, waiting for transfers between devices: 183 us -> none  [the longest x1 95.7 us: per_device(): lax.all_gather(w_query, 'ctx', axis=0, tiled=True)]
    all_to_all x1 -> x0, blocking collectives: 90.1 us -> none  [per_device(): lax.all_to_all(halves, 'ctx', split_axis=0, concat_axis=0, tiled=True)]
    all_to_all x1 -> x0, waiting for transfers between devices: 82.7 us -> none  [per_device(): lax.all_to_all(pair_sum, 'ctx', split_axis=0, concat_axis=0, tiled=True)]
    dot_general x15 -> x5, matrix products: 84.7 us -> 36 us  [the longest x1 22.2 us: per_device(): jnp.dot(hidden, w_down[0], preferred_element_type=f32).astype(bf16)]
    gather x2 -> x0, local copies, waits for them, and re-layouts: 17.4 us -> none  [per_device(): jnp.take(summed, targets, axis=0).reshape(tok_rows, TOP, model_width)]
    reduce_sum x12 -> x1, other arithmetic: 16.1 us -> 0.02 us  [per_device(): jnp.sum(jnp.where(member, route_weights[:, :, None], 0.0), axis=1)]
    while x12 -> x0, local copies, waits for them, and re-layouts: 12.8 us -> none
  transfers between devices with their start and end apart: 7 -> 0, of which waited for: 7 -> 0; matrix products, arithmetic and copies ran while one was open for 12% -> 0% of each run, Pallas kernels for 0% -> 0%
where the time goes in v1:
time: 372 us; the launch traced here: 368 us
  Pallas kernels  286 us (77%)
  matrix products  36 us (10%)
  local copies, waits for them, and re-layouts  32.6 us (9%)
  other arithmetic  13.5 us (4%)
    pallas_call x4, Pallas kernels, call(): pl.pallas_call(functools.partial(kernel, chips), out_shape=out_shape, in_...  286 us
    dot_general x1, matrix products, per_device(): jnp.dot(hidden, w_down[0], preferred_element_type=f32).astype(bf16)  22.2 us
    dot_general x1, matrix products, per_device(): up_val = jnp.dot(packed, w_up[0], preferred_element_type=f32)  11.2 us
    convert_element_type x1, local copies, waits for them, and re-layouts, per_device(): jnp.dot(hidden, w_down[0], preferred_element_type=f32).astype(bf16)  10.5 us

profile of v1, /device:TPU:15, one launch (start us, length us, event | category | flops | bytes accessed | tf_op | source)
XLA Modules:
  0.0 368.2 jit_solution(7929125658691963567)
XLA Ops:
  0.2 1.6 fusion.15
  1.8 1.6 fusion.17
  3.4 0.7 fusion.31
  4.2 1.8 convolution_convert_fusion.1
  6.1 0.7 pad_maximum_fusion.kv
  6.9 1.3 copy.56
  8.4 0.6 maximum_bitcast_fusion.meta
  9.0 78.3 %shard_map.136 = (f32[128,2048]{1,0:T(8,128)}, bf16[16,128,512]{2,1,0:T(8,128)(2,1)}, f32[16,16,128]{2,1,0:T(8,128)}) custom-call(bf16[16,128,180]{2,1,0:T(8,128)(2,1)} %bitcast.48, bf16[128,512]{1,0:T(8,128)(2,1)} %pad_maximum_fusion.kv, f32[16,128]{1,0:T(8,128)} %maximum_bitcast_fusion.meta, bf16[180,2048]{1,0:T(8,128)(2,1)} %weight.2), custom_call_target="tpu_custom_call" | custom-call | tf_op jit(solution)/shard_map/pallas_call | solution.py:329
  87.3 1.5 copy.59
  89.0 0.6 copy.75
  89.6 1.9 copy.76
  91.7 2.2 subtract_convert_fusion
  93.9 1.6 fusion.19.query
  95.5 3.6 reshape.144
  99.2 2.7 copy.78
  101.9 2.3 slice_bitcast_fusion
  104.5 0.7 copy.66.start
  105.2 1.2 copy.67.weight
  106.4 1.2 copy.68.tokens
  107.5 74.2 %shard_map.137 = f32[128,2880]{1,0:T(8,128)} custom-call(bf16[32,128,64]{2,1,0:T(8,128)(2,1)} %fusion.19.query, bf16[4,2048,64]{2,1,0:T(8,128)(2,1)} %get-tuple-element.16.key, bf16[4,2048,64]{2,1,0:T(8,128)(2,1)} %get-tuple-element.15.value, f32[32]{0:T(128)} %sinks.1, s32[128,1]{1,0:T(8,128)} %copy.66.start, bf16[128,2880]{1,0:T(8,128)(2,1)} %copy.67.weight, ...), custom_call_target="tpu_custom_call" | custom-call | tf_op jit(solution)/shard_map/pallas_call | solution.py:329
  181.8 1.6 fusion.12
  183.4 1.1 fusion.14.rows_in
  184.5 0.9 constant_dynamic-slice_fusion
  185.4 0.9 compare_convert_fusion.1.select
  186.3 67.0 %shard_map.138 = bf16[16,80,2880]{2,1,0:T(8,128)(2,1)} custom-call(bf16[128,2880]{1,0:T(8,128)(2,1)} %fusion.14.rows_in, bf16[16,80,128]{2,1,0:T(8,128)(2,1)} %compare_convert_fusion.1.select), custom_call_target="tpu_custom_call" | custom-call | tf_op jit(solution)/shard_map/pallas_call | solution.py:329
  253.3 11.2 %fusion.3 = f32[1280,768]{1,0:T(8,128)} fusion(bf16[1280,2880]{1,0:T(8,128)(2,1)} %bitcast.46, bf16[1,2880,768]{2,1,0:T(8,128)(2,1)} %param.26), kind=kOutput, calls=%fused_computation.4 | convolution fusion | flops 5662310400 | bytes 15728640 | tf_op jit(solution)/shard_map/dot_general | solution.py:435
  264.4 22.2 %convolution_convert_fusion = bf16[1280,2880]{0,1:T(8,128)(2,1)} fusion(bf16[1,768,2880]{1,2,0:T(8,128)(2,1)} %param.27, bf16[1280,2880]{1,0:T(8,128)(2,1)} %bitcast.47, bf16[1,2880,768]{2,1,0:T(8,128)(2,1)} %param.25, f32[1280,768]{1,0:T(8,128)} %fusion.3), kind=kOutput, calls=%fused_computation | convolution fusion | flops 11336171520 | bytes 27525120 | tf_op jit(solution)/shard_map/dot_general | solution.py:437
  286.6 10.5 %copy.69 = bf16[1280,2880]{1,0:T(8,128)(2,1)} copy(bf16[1280,2880]{0,1:T(8,128)(2,1)} %convolution_convert_fusion) | data formatting | bytes 14745600 | tf_op jit(solution)/shard_map/convert_element_type | solution.py:437
  297.1 1.4 copy.70.weights
  298.5 1.1 compare_convert_fusion.select
  299.6 66.3 %shard_map.139 = bf16[128,2880]{1,0:T(8,128)(2,1)} custom-call(bf16[16,80,2880]{2,1,0:T(8,128)(2,1)} %bitcast.44, bf16[16,128,80]{2,1,0:T(8,128)(2,1)} %compare_convert_fusion.select, f32[16,128,1]{2,1,0:T(8,128)} %copy.70.weights, bf16[128,2880]{1,0:T(8,128)(2,1)} %copy-done), custom_call_target="tpu_custom_call" | custom-call | tf_op jit(solution)/shard_map/pallas_call | solution.py:329
  365.9 2.3 copy.71
  (36 shorter events, 1.2 us)
Async XLA Ops:
  0.0 3.4 copy-start.3
  6.1 2.1 copy-start.6
  6.1 2.3 copy-start.7
  93.9 1.6 copy-start.2
  101.9 2.3 copy-start.8
  101.9 3.3 copy-start.4
  101.9 4.4 %copy-start.1 = (bf16[128,2880]{0,1:T(8,128)(2,1)S(1)}, bf16[128,2880]{0,1:T(8,128)(2,1)}, u32[]{:S(2)}) copy-start(bf16[128,2880]{0,1:T(8,128)(2,1)} %param.14) | copy-start | bytes 2211844
  181.7 1.6 copy-start.5
  183.4 69.9 %copy-start = (bf16[128,2880]{1,0:T(8,128)(2,1)}, bf16[128,2880]{1,0:T(8,128)(2,1)S(1)}, u32[]{:S(2)}) copy-start(bf16[128,2880]{1,0:T(8,128)(2,1)S(1)} %get-tuple-element.12.mixed) | copy-start | bytes 2211844

commit v2 on v1

--- a/solution.py
+++ b/solution.py
@@ -37,9 +37,12 @@
         else:
             self.pos = chip
         self.way = 1 - 2 * self.core
-        self.partner = self.me + self.way
-        self.next = self.owner(-1)
-        self.prev = self.owner(1)
+        self.partner = {"ctx": self.me + self.way}
+        self.next = {"ctx": self.owner(-1)}
+        self.prev = {"ctx": self.owner(1)}
+        group = lax.axis_index("groups")
+        self.parity = lax.rem(group, 2)
+        self.peer = {"groups": group + 1 - 2 * self.parity}
 
     def index(self, pos, core):
         pos = lax.rem(pos + 2 * self.chips, self.chips)
@@ -57,85 +60,109 @@
     def partner_owner(self, step):
         return self.index(self.pos + self.way * step, 1 - self.core)
 
-    def barrier(self):
+    def barrier(self, with_peer=False):
         sem = pltpu.get_barrier_semaphore()
-        for other in (self.next, self.prev, self.partner):
-            pl.semaphore_signal(sem, inc=1, device_id={"ctx": other}, device_id_type=MESH)
-        pl.semaphore_wait(sem, 3)
-
-
-def gather_ring(ring, pieces, sems, work):
-    ring_send, ring_recv, part_send, part_recv = sems
+        others = [self.next, self.prev, self.partner] + ([self.peer] if with_peer else [])
+        for other in others:
+            pl.semaphore_signal(sem, inc=1, device_id=other, device_id_type=MESH)
+        pl.semaphore_wait(sem, len(others))
+
+
+def gather_ring(ring, pieces, sems, setup, work):
+    ring_send, ring_recv, part_send, part_recv, peer_send, peer_recv = sems
     chips = ring.chips
-
-    def copies(i, step, own):
-        source, slots, view = pieces[i]
-        who = ring.owner(step)
-        src = view(source) if own else view(slots.at[who])
-        out = []
-        for target, send, recv in (
-            (ring.next, ring_send, ring_recv),
-            (ring.partner, part_send, part_recv),
-        ):
-            at = step + 1 if target is ring.next else step
-            out.append(
-                pltpu.make_async_remote_copy(
-                    src_ref=src,
-                    dst_ref=view(slots.at[who]),
-                    send_sem=send.at[i, step],
-                    recv_sem=recv.at[i, at],
-                    device_id={"ctx": target},
-                    device_id_type=MESH,
-                )
-            )
-        return out
-
-    def arrived(i, step, recv, who):
-        slots, view = pieces[i][1], pieces[i][2]
-        ref = view(slots.at[who])
-        pltpu.make_async_copy(ref, ref, recv.at[i, step]).wait()
-
-    ring.barrier()
+    ringed = [i for i, piece in enumerate(pieces) if piece[3] != "peer"]
+    peered = [i for i, piece in enumerate(pieces) if piece[3] == "peer"]
+    shared = [i for i, piece in enumerate(pieces) if piece[3] == "both"]
+    lag = 2 if peered else 1
+
+    def copy(i, step, target, send, recv, own=False):
+        source, slots, view, _ = pieces[i]
+        dst = view(slots.at[ring.owner(step)])
+        return pltpu.make_async_remote_copy(
+            src_ref=view(source) if own else dst,
+            dst_ref=dst,
+            send_sem=send,
+            recv_sem=recv,
+            device_id=target,
+            device_id_type=MESH,
+        )
+
+    def onward(i, step, own=False):
+        return copy(
+            i, step, ring.next, ring_send.at[i, step], ring_recv.at[i, step + 1], own
+        )
+
+    def across(i, step, own=False):
+        return copy(i, step, ring.partner, part_send.at[i, step], part_recv.at[i, step], own)
+
+    def aside(i, step):
+        return copy(i, step, ring.peer, peer_send.at[step], peer_recv.at[step])
+
+    def arrived(i, sem, who):
+        ref = pieces[i][2](pieces[i][1].at[who])
+        pltpu.make_async_copy(ref, ref, sem).wait()
+
+    ring.barrier(bool(peered))
+    for i in ringed:
+        onward(i, 0, True).start()
     for i in range(len(pieces)):
-        for copy in copies(i, 0, True):
-            copy.start()
-    for source, slots, view in pieces:
-        view(slots.at[ring.me])[...] = view(source)[...]
-    work(ring.me)
-
-    def step(s, carry):
-        who = ring.owner(s)
+        across(i, 0, True).start()
+    filled = []
+    for source, slots, _, _ in pieces:
+        if not any(slots is other for other in filled):
+            slots[ring.me] = source[...]
+            filled.append(slots)
+    setup()
+
+    def turn(t, carry):
+        @pl.when(t < chips)
+        def _():
+            for i in ringed:
+                arrived(i, ring_recv.at[i, t], ring.owner(t))
+
+                @pl.when(t < chips - 1)
+                def _():
+                    onward(i, t).start()
+
+                if i in shared:
+                    aside(i, t).start()
+                across(i, t).start()
+
+        if peered:
+
+            @pl.when((t > 1) & (t <= chips))
+            def _():
+                for i in peered:
+                    arrived(i, peer_recv.at[t - 1], ring.owner(t - 1))
+                    across(i, t - 1).start()
+
+        @pl.when(t >= lag)
+        def _():
+            s = t - lag
+            for i in range(len(pieces)):
+                arrived(i, part_recv.at[i, s], ring.partner_owner(s))
+            work(s)
+
+        return carry
+
+    lax.fori_loop(1, chips + lag, turn, 0)
+
+    def drain(s, carry):
         for i in range(len(pieces)):
-            arrived(i, s, ring_recv, who)
-            onward, across = copies(i, s, False)
+            across(i, s).wait_send()
+        for i in ringed:
 
             @pl.when(s < chips - 1)
             def _():
-                onward.start()
-
-            across.start()
-        work(who)
-        late = ring.partner_owner(s - 1)
-        for i in range(len(pieces)):
-            arrived(i, s - 1, part_recv, late)
-        work(late)
-        return carry
-
-    lax.fori_loop(1, chips, step, 0)
-    late = ring.partner_owner(chips - 1)
-    for i in range(len(pieces)):
-        arrived(i, chips - 1, part_recv, late)
-    work(late)
-
-    def drain(s, carry):
-        for i in range(len(pieces)):
-            onward, across = copies(i, s, False)
-
-            @pl.when(s < chips - 1)
+                onward(i, s).wait_send()
+
+        for i in shared:
+
+            @pl.when(s > 0)
             def _():
-                onward.wait_send()
-
-            across.wait_send()
+                aside(i, s).wait_send()
+
         return carry
 
     lax.fori_loop(0, chips, drain, 0)
@@ -145,6 +172,10 @@
     return [pltpu.SemaphoreType.DMA((count, chips))] * 4
 
 
+def gather_sems(count, chips):
+    return ring_sems(count, chips) + [pltpu.SemaphoreType.DMA((chips,))] * 2
+
+
 def whole(ref):
     return ref
 
@@ -157,39 +188,75 @@
     return lambda ref: ref.at[pl.ds(start, size), :]
 
 
+def thirds(ring, source, slots):
+    width = source.shape[1]
+    third = width // 3 // 128 * 128
+    mine = pl.multiple_of(ring.parity * third, 128)
+    other = pl.multiple_of((1 - ring.parity) * third, 128)
+    return [
+        (source, slots, cols(mine, third), "both"),
+        (source, slots, cols(2 * third, width - 2 * third), "ring"),
+        (source, slots, cols(other, third), "peer"),
+    ]
+
+
 def query_kernel(chips, lhs, kv, meta, weight, out, kv_all, meta_all, slots, *sems):
     ring = Ring(chips)
-    half = weight.shape[1] // 2
-    pieces = [
-        (kv, kv_all, whole),
-        (meta, meta_all, whole),
-        (weight, slots, cols(0, half)),
-        (weight, slots, cols(half, half)),
-    ]
-    out[...] = jnp.zeros_like(out)
-
-    def work(who):
-        out[...] += jnp.dot(lhs[who], slots[who], preferred_element_type=jnp.float32)
-
-    gather_ring(ring, pieces, sems, work)
+    pieces = [(kv, kv_all, whole, "ring"), (meta, meta_all, whole, "ring")]
+    pieces += thirds(ring, weight, slots)
+
+    def setup():
+        out[...] = jnp.zeros_like(out)
+
+    def work(s):
+        for who in (ring.owner(s), ring.partner_owner(s)):
+            out[...] += jnp.dot(lhs[who], slots[who], preferred_element_type=jnp.float32)
+
+    gather_ring(ring, pieces, sems, setup, work)
 
 
 def attend_kernel(
-    chips, query, key, value, sinks, start, weight, tokens, out, slots, bias, attended, *sems
+    chips, raw, kv_all, cosine, sine, sinks, start, weight, tokens,
+    out, slots, bias, query, key, value, attended, *sems
 ):
     ring = Ring(chips)
     blocks, tok_rows, width = attended.shape
     per_block = width // HD
-    seq = key.shape[1]
-    group = query.shape[0] // key.shape[0]
-    half = weight.shape[0] // 2
-    pieces = [(weight, slots, rows(0, half)), (weight, slots, rows(half, half))]
-    key_pos = lax.broadcasted_iota(jnp.int32, (tok_rows, seq), 1)
-    row_pos = lax.broadcasted_iota(jnp.int32, (tok_rows, seq), 0) + ring.me * tok_rows
-    allowed = (key_pos <= row_pos) & (key_pos >= start[...])
-    bias[...] = jnp.where(allowed, 0.0, NEGATIVE)
-
-    def work(who):
+    kv_heads, seq, _ = key.shape
+    group = query.shape[0] // kv_heads
+    pieces = thirds(ring, weight, slots)
+
+    def setup():
+        key_pos = lax.broadcasted_iota(jnp.int32, (tok_rows, seq), 1)
+        row_pos = lax.broadcasted_iota(jnp.int32, (tok_rows, seq), 0) + ring.me * tok_rows
+        allowed = (key_pos <= row_pos) & (key_pos >= start[...])
+        bias[...] = jnp.where(allowed, 0.0, NEGATIVE)
+        lane = lax.broadcasted_iota(jnp.int32, (tok_rows, 2 * HD), 1)
+        first = lax.rem(lane, HD) < HD // 2
+
+        def turn_pair(j, carry):
+            pair = raw[:, pl.ds(pl.multiple_of(j * 2 * HD, 2 * HD), 2 * HD)]
+            other = jnp.where(
+                first, pltpu.roll(pair, 2 * HD - HD // 2, 1), pltpu.roll(pair, HD // 2, 1)
+            )
+            turned = ((pair * cosine[...] + other * sine[...]) * SCALE).astype(jnp.bfloat16)
+            query[2 * j] = turned[:, :HD]
+            query[2 * j + 1] = turned[:, HD:]
+            return carry
+
+        lax.fori_loop(0, query.shape[0] // 2, turn_pair, 0)
+
+        def unpack(d, carry):
+            at = pl.ds(pl.multiple_of(d * tok_rows, tok_rows), tok_rows)
+            block = kv_all[d]
+            for g in range(kv_heads):
+                key[g, at, :] = block[:, g * HD : (g + 1) * HD]
+                value[g, at, :] = block[:, (kv_heads + g) * HD : (kv_heads + g + 1) * HD]
+            return carry
+
+        lax.fori_loop(0, blocks, unpack, 0)
+
+    def attend(who):
         heads = []
         for j in range(per_block):
             head = who * per_block + j
@@ -214,7 +281,11 @@
         joined = heads[0] if per_block == 1 else jnp.concatenate(heads, axis=1)
         attended[who] = joined.astype(jnp.bfloat16)
 
-    gather_ring(ring, pieces, sems, work)
+    def work(s):
+        attend(ring.owner(s))
+        attend(ring.partner_owner(s))
+
+    gather_ring(ring, pieces, sems, setup, work)
     out[...] = tokens[...].astype(jnp.float32)
 
     def project(d, carry):
@@ -224,17 +295,50 @@
     lax.fori_loop(0, blocks, project, 0)
 
 
-def dispatch_kernel(chips, rows_in, select, out, slots, *sems):
+def expert_kernel(
+    chips, rows_in, select, w_gate, w_up, w_down,
+    out, slots, packed, gate, up, down, load_sem, *sems
+):
     ring = Ring(chips)
     half = rows_in.shape[0] // 2
-    pieces = [(rows_in, slots, rows(0, half)), (rows_in, slots, rows(half, half))]
-
-    def work(who):
-        out[who] = jnp.dot(select[who], slots[who], preferred_element_type=jnp.float32).astype(
-            jnp.bfloat16
-        )
-
-    gather_ring(ring, pieces, sems, work)
+    padded = select.shape[1]
+    pieces = [
+        (rows_in, slots, rows(0, half), "ring"),
+        (rows_in, slots, rows(half, half), "ring"),
+    ]
+    loads = [
+        pltpu.make_async_copy(source, target, load_sem.at[i])
+        for i, (source, target) in enumerate(((w_gate, gate), (w_up, up), (w_down, down)))
+    ]
+    for load in loads:
+        load.start()
+
+    def work(s):
+        whose = [
+            ring.owner(s - 1), ring.partner_owner(s - 1), ring.owner(s), ring.partner_owner(s)
+        ]
+
+        @pl.when(s == 1)
+        def _():
+            for load in loads:
+                load.wait()
+
+        @pl.when(lax.rem(s, 2) == 1)
+        def _():
+            for j, who in enumerate(whose):
+                packed[j * padded : (j + 1) * padded, :] = jnp.dot(
+                    select[who], slots[who], preferred_element_type=jnp.float32
+                ).astype(jnp.bfloat16)
+            gate_val = jnp.dot(packed[...], gate[...], preferred_element_type=jnp.float32)
+            up_val = jnp.dot(packed[...], up[...], preferred_element_type=jnp.float32)
+            hidden = (up_val + 1.0) * gate_val * jax.nn.sigmoid(ALPHA * gate_val)
+            partial = jnp.dot(
+                hidden.astype(jnp.bfloat16), down[...], preferred_element_type=jnp.float32
+            ).astype(jnp.bfloat16)
+            for j, who in enumerate(whose):
+                out[who] = partial[j * padded : (j + 1) * padded, :]
+
+    gather_ring(ring, pieces, sems, lambda: None, work)
 
 
 def combine_kernel(
@@ -258,7 +362,7 @@
             dst_ref=cross_in.at[s, at, :],
             send_sem=part_send.at[h, s],
             recv_sem=part_recv.at[h, s],
-            device_id={"ctx": ring.partner},
+            device_id=ring.partner,
             device_id_type=MESH,
         )
 
@@ -269,7 +373,7 @@
             dst_ref=ring_in.at[s, at, :],
             send_sem=ring_send.at[h, s],
             recv_sem=ring_recv.at[h, s],
-            device_id={"ctx": ring.next},
+            device_id=ring.next,
             device_id_type=MESH,
         )
 
@@ -324,13 +428,18 @@
     lax.fori_loop(0, chips, drain, 0)
 
 
-def call(kernel, chips, out_shape, scratch, identity, *args, smem=()):
+def call(kernel, chips, out_shape, scratch, identity, *args, smem=(), hbm=()):
     single = not isinstance(out_shape, (list, tuple))
     return pl.pallas_call(
         functools.partial(kernel, chips),
         out_shape=out_shape,
         in_specs=[
-            pl.BlockSpec(memory_space=pltpu.SMEM) if i in smem else VMEM for i in range(len(args))
+            pl.BlockSpec(memory_space=pltpu.SMEM)
+            if i in smem
+            else pl.BlockSpec(memory_space=pl.ANY)
+            if i in hbm
+            else VMEM
+            for i in range(len(args))
         ],
         out_specs=VMEM if single else [VMEM] * len(out_shape),
         scratch_shapes=scratch,
@@ -390,13 +499,12 @@
             jax.ShapeDtypeStruct((devices,) + kv.shape, bf16),
             jax.ShapeDtypeStruct((devices,) + meta.shape, f32),
         ],
-        [pltpu.VMEM((devices,) + w_query.shape, bf16)] + ring_sems(4, chips),
+        [pltpu.VMEM((devices,) + w_query.shape, bf16)] + gather_sems(5, chips),
         0,
         lhs, kv, meta, w_query,
     )
-    query = rotate(raw_query.reshape(tok_rows, num_heads, HD)) * SCALE
-    query = query.astype(bf16).transpose(1, 0, 2)
-    halves = kv_all.reshape(devices * tok_rows, 2, kv_heads, HD).transpose(1, 2, 0, 3)
+    cosine_pair = jnp.tile(cosine[:, 0, :], (1, 4))
+    sine_pair = jnp.tile(jnp.concatenate([-sine[:, 0, :], sine[:, 0, :]], axis=1), (1, 2))
     doc_ends = jnp.cumsum(lengths)
     start = jnp.max(
         jnp.where(positions[:, None] >= doc_ends[None, :], doc_ends[None, :], 0), axis=1
@@ -408,12 +516,15 @@
         [
             pltpu.VMEM((devices,) + w_out.shape, bf16),
             pltpu.VMEM((tok_rows, devices * tok_rows), f32),
+            pltpu.VMEM((num_heads, tok_rows, HD), bf16),
+            pltpu.VMEM((kv_heads, devices * tok_rows, HD), bf16),
+            pltpu.VMEM((kv_heads, devices * tok_rows, HD), bf16),
             pltpu.VMEM((devices, tok_rows, w_out.shape[0]), bf16),
         ]
-        + ring_sems(2, chips),
+        + gather_sems(3, chips),
         1,
-        query, halves[0], halves[1], sinks, start, w_out, tokens,
-        smem=(3,),
+        raw_query, kv_all, cosine_pair, sine_pair, sinks, start, w_out, tokens,
+        smem=(4,),
     )
     mixed = projected.astype(bf16)
     expert_in = rms_scale(mixed, moe_gain)
@@ -423,18 +534,23 @@
     places = jnp.arange(padded, dtype=jnp.int32).astype(f32)
     select = (slot_all[:, None, :] == places[None, :, None]).astype(bf16)
     select_back = (slot_all[:, :, None] == places[None, None, :]).astype(bf16)
-    packed = call(
-        dispatch_kernel,
+    partial = call(
+        expert_kernel,
         chips,
         jax.ShapeDtypeStruct((devices, padded, width), bf16),
-        [pltpu.VMEM((devices, tok_rows, width), bf16)] + ring_sems(2, chips),
+        [
+            pltpu.VMEM((devices, tok_rows, width), bf16),
+            pltpu.VMEM((4 * padded, width), bf16),
+            pltpu.VMEM(w_gate.shape[1:], bf16),
+            pltpu.VMEM(w_up.shape[1:], bf16),
+            pltpu.VMEM(w_down.shape[1:], bf16),
+            pltpu.SemaphoreType.DMA((3,)),
+        ]
+        + gather_sems(2, chips),
         2,
-        expert_in, select,
-    ).reshape(devices * padded, width)
-    gate_val = jnp.dot(packed, w_gate[0], preferred_element_type=f32)
-    up_val = jnp.dot(packed, w_up[0], preferred_element_type=f32)
-    hidden = ((up_val + 1.0) * gate_val * jax.nn.sigmoid(ALPHA * gate_val)).astype(bf16)
-    partial = jnp.dot(hidden, w_down[0], preferred_element_type=f32).astype(bf16)
+        expert_in, select, w_gate[0], w_up[0], w_down[0],
+        hbm=(2, 3, 4),
+    )
     return call(
         combine_kernel,
         chips,
@@ -443,7 +559,7 @@
         + [pltpu.VMEM((chips - 1, tok_rows, width), bf16)] * 2
         + ring_sems(2, chips),
         3,
-        partial.reshape(devices, padded, width), select_back, weight_all[:, :, None], mixed,
+        partial, select_back, weight_all[:, :, None], mixed,
     )
 
 

time: 372 us -> 297 us (0.80)
  matrix products: 36 us -> 2.68 us
  Pallas kernels: 286 us -> 263 us
  local copies, waits for them, and re-layouts: 32.6 us -> 17.2 us
  other arithmetic: 13.5 us -> 9.71 us
    dot_general x2 -> x0, matrix products: 33.3 us -> none  [the longest x1 22.2 us: per_device(): jnp.dot(hidden, w_down[0], preferred_element_type=f32).astype(bf16)]
    pallas_call x4, Pallas kernels: 286 us -> 263 us  [call(): pl.pallas_call(functools.partial(kernel, chips), out_shape=out_shape, in_...]
    convert_element_type x1 -> x0, local copies, waits for them, and re-layouts: 10.5 us -> none  [per_device(): jnp.dot(hidden, w_down[0], preferred_element_type=f32).astype(bf16)]
    reshape x2 -> x0, local copies, waits for them, and re-layouts: 6.36 us -> none  [per_device(): kv_all.reshape(devices * tok_rows, 2, kv_heads, HD).transpose(1, 2, 0, 3)]
    unnamed x22 -> x19, local copies, waits for them, and re-layouts: 4.89 us -> 8.92 us
where the time goes in v2:
time: 297 us; the launch traced here: 293 us
  Pallas kernels  263 us (89%)
  local copies, waits for them, and re-layouts  17.2 us (6%)
  other arithmetic  9.71 us (3%)
    pallas_call x4, Pallas kernels, call(): pl.pallas_call(functools.partial(kernel, chips), out_shape=out_shape, in_...  263 us
    unnamed x19, local copies, waits for them, and re-layouts  8.92 us

profile of v2, /device:TPU:15, one launch (start us, length us, event | category | flops | bytes accessed | tf_op | source)
XLA Modules:
  0.0 292.8 jit_solution(12405724018711094259)
XLA Ops:
  0.0 0.1 fusion.12
  0.2 1.6 fusion.3
  1.8 1.6 fusion.5
  3.4 0.7 fusion.16
  4.1 0.1 copy.37
  4.2 1.8 convolution_convert_fusion
  6.1 0.7 pad_maximum_fusion.kv
  6.8 0.1 reshape.158
  6.9 1.3 copy.35
  8.2 0.1 fusion.6
  8.4 0.6 maximum_bitcast_fusion.meta
  9.0 62.6 %shard_map.136 = (f32[128,2048]{1,0:T(8,128)}, bf16[16,128,512]{2,1,0:T(8,128)(2,1)}, f32[16,16,128]{2,1,0:T(8,128)}) custom-call(bf16[16,128,180]{2,1,0:T(8,128)(2,1)} %bitcast.25, bf16[128,512]{1,0:T(8,128)(2,1)} %pad_maximum_fusion.kv, f32[16,128]{1,0:T(8,128)} %maximum_bitcast_fusion.meta, bf16[180,2048]{1,0:T(8,128)(2,1)} %weight.2), custom_call_target="tpu_custom_call" | custom-call | tf_op jit(solution)/shard_map/pallas_call | solution.py:433
  71.6 0.0 copy-start.1
  71.7 0.7 copy.39.sine
  72.4 0.7 copy.38.cosine
  73.1 0.2 reduce-window.8
  73.3 0.1 select_reduce_fusion.1
  73.4 0.7 copy.40.start
  74.1 1.2 copy.41.weight
  75.3 1.2 copy.42.tokens
  76.5 60.6 %shard_map.137 = f32[128,2880]{1,0:T(8,128)} custom-call(f32[128,2048]{1,0:T(8,128)} %get-tuple-element.8.raw, bf16[16,128,512]{2,1,0:T(8,128)(2,1)} %get-tuple-element.9.kv_all, f32[128,128]{1,0:T(8,128)} %copy.38.cosine, f32[128,128]{1,0:T(8,128)} %copy.39.sine, f32[32]{0:T(128)} %sinks.1, s32[128,1]{1,0:T(8,128)} %copy.40.start, ...), custom_call_target="tpu_custom_call" | custom-call | tf_op jit(solution)/shard_map/pallas_call | solution.py:433
  137.1 0.0 copy-start.4
  137.1 1.6 fusion
  138.8 1.2 fusion.2.rows_in
  139.9 0.9 constant_dynamic-slice_fusion
  140.8 0.9 compare_convert_fusion.1.select
  141.7 6.6 %copy.43 = bf16[1,768,2880]{2,1,0:T(8,128)(2,1)} copy(bf16[1,768,2880]{1,2,0:T(8,128)(2,1)} %param.27) | data formatting | bytes 8847360 | tf_op args[13]
  148.3 73.9 %shard_map.138.partial = bf16[16,80,2880]{2,1,0:T(8,128)(2,1)} custom-call(bf16[128,2880]{1,0:T(8,128)(2,1)} %fusion.2.rows_in, bf16[16,80,128]{2,1,0:T(8,128)(2,1)} %compare_convert_fusion.1.select, bf16[2880,768]{1,0:T(8,128)(2,1)} %bitcast.23, bf16[2880,768]{1,0:T(8,128)(2,1)} %bitcast.24, bf16[768,2880]{1,0:T(8,128)(2,1)} %bitcast.22), custom_call_target="tpu_custom_call" | custom-call | tf_op jit(solution)/shard_map/pallas_call | solution.py:433
  222.1 1.4 copy.44.weights
  223.5 1.1 compare_convert_fusion.select
  224.6 65.9 %shard_map.139 = bf16[128,2880]{1,0:T(8,128)(2,1)} custom-call(bf16[16,80,2880]{2,1,0:T(8,128)(2,1)} %shard_map.138.partial, bf16[16,128,80]{2,1,0:T(8,128)(2,1)} %compare_convert_fusion.select, f32[16,128,1]{2,1,0:T(8,128)} %copy.44.weights, bf16[128,2880]{1,0:T(8,128)(2,1)} %copy-done), custom_call_target="tpu_custom_call" | custom-call | tf_op jit(solution)/shard_map/pallas_call | solution.py:433
  290.5 2.3 copy.45
  (26 shorter events, 0.1 us)
Async XLA Ops:
  0.0 3.4 %copy-start.2 = (bf16[2880,256]{1,0:T(8,128)(2,1)S(1)}, bf16[2880,256]{1,0:T(8,128)(2,1)}, u32[]{:S(2)}) copy-start(bf16[2880,256]{1,0:T(8,128)(2,1)} %param.18) | copy-start | bytes 4423684
  6.7 1.5 copy-start.5
  6.7 1.6 copy-start.6
  8.2 64.9 %copy-start.7 = (s32[4]{0:T(128)S(1)}, s32[4]{0:T(128)}, u32[]{:S(2)}) copy-start(s32[4]{0:T(128)} %param.15) | copy-start | bytes 52
  8.2 65.9 %copy-start.3 = (bf16[128,2880]{0,1:T(8,128)(2,1)S(1)}, bf16[128,2880]{0,1:T(8,128)(2,1)}, u32[]{:S(2)}) copy-start(bf16[128,2880]{0,1:T(8,128)(2,1)} %param.21) | copy-start | bytes 2211844
  71.6 3.7 %copy-start.1 = (bf16[128,2880]{0,1:T(8,128)(2,1)S(1)}, bf16[128,2880]{0,1:T(8,128)(2,1)}, u32[]{:S(2)}) copy-start(bf16[128,2880]{0,1:T(8,128)(2,1)} %param.14) | copy-start | bytes 2211844
  137.1 1.6 copy-start.4
  138.7 9.5 %copy-start = (bf16[128,2880]{1,0:T(8,128)(2,1)}, bf16[128,2880]{1,0:T(8,128)(2,1)S(1)}, u32[]{:S(2)}) copy-start(bf16[128,2880]{1,0:T(8,128)(2,1)S(1)} %get-tuple-element.12.mixed) | copy-start | bytes 2211844

commit v3 on v2

--- a/solution.py
+++ b/solution.py
@@ -216,8 +216,8 @@
 
 
 def attend_kernel(
-    chips, raw, kv_all, cosine, sine, sinks, start, weight, tokens,
-    out, slots, bias, query, key, value, attended, *sems
+    chips, raw, kv_all, cosine, sine, sinks, start, weight, tokens, gain,
+    mixed_out, expert_in, out, slots, bias, query, key, value, attended, *sems
 ):
     ring = Ring(chips)
     blocks, tok_rows, width = attended.shape
@@ -293,6 +293,8 @@
         return carry
 
     lax.fori_loop(0, blocks, project, 0)
+    mixed_out[...] = out[...].astype(jnp.bfloat16)
+    expert_in[...] = rms_scale(mixed_out[...], gain[...])
 
 
 def expert_kernel(
@@ -332,8 +334,11 @@
             gate_val = jnp.dot(packed[...], gate[...], preferred_element_type=jnp.float32)
             up_val = jnp.dot(packed[...], up[...], preferred_element_type=jnp.float32)
             hidden = (up_val + 1.0) * gate_val * jax.nn.sigmoid(ALPHA * gate_val)
-            partial = jnp.dot(
-                hidden.astype(jnp.bfloat16), down[...], preferred_element_type=jnp.float32
+            partial = lax.dot_general(
+                hidden.astype(jnp.bfloat16),
+                down[...],
+                (((1,), (1,)), ((), ())),
+                preferred_element_type=jnp.float32,
             ).astype(jnp.bfloat16)
             for j, who in enumerate(whose):
                 out[who] = partial[j * padded : (j + 1) * padded, :]
@@ -509,11 +514,12 @@
     start = jnp.max(
         jnp.where(positions[:, None] >= doc_ends[None, :], doc_ends[None, :], 0), axis=1
     )[:, None]
-    projected = call(
+    mixed, expert_in = call(
         attend_kernel,
         chips,
-        jax.ShapeDtypeStruct((tok_rows, width), f32),
+        [jax.ShapeDtypeStruct((tok_rows, width), bf16)] * 2,
         [
+            pltpu.VMEM((tok_rows, width), f32),
             pltpu.VMEM((devices,) + w_out.shape, bf16),
             pltpu.VMEM((tok_rows, devices * tok_rows), f32),
             pltpu.VMEM((num_heads, tok_rows, HD), bf16),
@@ -523,11 +529,9 @@
         ]
         + gather_sems(3, chips),
         1,
-        raw_query, kv_all, cosine_pair, sine_pair, sinks, start, w_out, tokens,
+        raw_query, kv_all, cosine_pair, sine_pair, sinks, start, w_out, tokens, moe_gain[None, :],
         smem=(4,),
     )
-    mixed = projected.astype(bf16)
-    expert_in = rms_scale(mixed, moe_gain)
     expert = me // 2
     slot_all = lax.dynamic_index_in_dim(meta_all, expert, 1, keepdims=False)
     weight_all = lax.dynamic_index_in_dim(meta_all, experts + expert, 1, keepdims=False)
@@ -543,12 +547,12 @@
             pltpu.VMEM((4 * padded, width), bf16),
             pltpu.VMEM(w_gate.shape[1:], bf16),
             pltpu.VMEM(w_up.shape[1:], bf16),
-            pltpu.VMEM(w_down.shape[1:], bf16),
+            pltpu.VMEM(w_down.shape[:0:-1], bf16),
             pltpu.SemaphoreType.DMA((3,)),
         ]
         + gather_sems(2, chips),
         2,
-        expert_in, select, w_gate[0], w_up[0], w_down[0],
+        expert_in, select, w_gate[0], w_up[0], w_down[0].T,
         hbm=(2, 3, 4),
     )
     return call(

time: 297 us -> 288 us (0.970)
  local copies, waits for them, and re-layouts: 17.2 us -> 11.2 us
    unnamed x19 -> x16, local copies, waits for them, and re-layouts: 8.92 us -> 2.33 us
where the time goes in v3:
time: 288 us; the launch traced here: 284 us
  Pallas kernels  263 us (91%)
  local copies, waits for them, and re-layouts  11.2 us (4%)
  other arithmetic  6.92 us (2%)
    pallas_call x4, Pallas kernels, call(): pl.pallas_call(functools.partial(kernel, chips), out_shape=out_shape, in_...  263 us

profile of v3, /device:TPU:15, one launch (start us, length us, event | category | flops | bytes accessed | tf_op | source)
XLA Modules:
  0.0 284.1 jit_solution(11113797683478609144)
XLA Ops:
  0.0 0.1 fusion.9
  0.2 1.6 fusion
  1.8 1.6 fusion.2
  3.4 0.0 copy-done.1
  3.4 0.7 fusion.13
  4.1 0.1 copy.35
  4.2 1.8 convolution_convert_fusion
  6.1 0.7 pad_maximum_fusion.kv
  6.8 0.1 reshape.149
  6.9 1.3 copy.33
  8.2 0.0 copy-done.4
  8.2 0.1 fusion.3
  8.4 0.6 maximum_bitcast_fusion.meta
  9.0 62.6 %shard_map.136 = (f32[128,2048]{1,0:T(8,128)}, bf16[16,128,512]{2,1,0:T(8,128)(2,1)}, f32[16,16,128]{2,1,0:T(8,128)}) custom-call(bf16[16,128,180]{2,1,0:T(8,128)(2,1)} %bitcast.27, bf16[128,512]{1,0:T(8,128)(2,1)} %pad_maximum_fusion.kv, f32[16,128]{1,0:T(8,128)} %maximum_bitcast_fusion.meta, bf16[180,2048]{1,0:T(8,128)(2,1)} %weight.2), custom_call_target="tpu_custom_call" | custom-call | tf_op jit(solution)/shard_map/pallas_call | solution.py:438
  71.6 0.0 copy-start
  71.7 0.7 copy.37.sine
  72.4 0.7 copy.36.cosine
  73.1 0.0 copy-done.6
  73.1 0.2 reduce-window.8
  73.3 0.1 select_reduce_fusion.1
  73.4 0.7 copy.38.start
  74.1 1.2 copy.39.weight
  75.3 1.1 copy.40.tokens
  76.4 0.6 broadcast_in_dim.62.gain
  77.0 60.8 %shard_map.137 = (bf16[128,2880]{1,0:T(8,128)(2,1)}, bf16[128,2880]{1,0:T(8,128)(2,1)}) custom-call(f32[128,2048]{1,0:T(8,128)} %get-tuple-element.10.raw, bf16[16,128,512]{2,1,0:T(8,128)(2,1)} %get-tuple-element.11.kv_all, f32[128,128]{1,0:T(8,128)} %copy.36.cosine, f32[128,128]{1,0:T(8,128)} %copy.37.sine, f32[32]{0:T(128)} %sinks.1, ...), custom_call_target="tpu_custom_call" | custom-call | tf_op jit(solution)/shard_map/pallas_call | solution.py:438
  137.9 0.9 constant_dynamic-slice_fusion
  138.8 0.9 compare_convert_fusion.1.select
  139.6 73.8 %shard_map.138.partial = bf16[16,80,2880]{2,1,0:T(8,128)(2,1)} custom-call(bf16[128,2880]{1,0:T(8,128)(2,1)} %get-tuple-element.12.rows_in, bf16[16,80,128]{2,1,0:T(8,128)(2,1)} %compare_convert_fusion.1.select, bf16[2880,768]{1,0:T(8,128)(2,1)} %bitcast.24, bf16[2880,768]{1,0:T(8,128)(2,1)} %bitcast.25, bf16[2880,768]{1,0:T(8,128)(2,1)} %bitcast.26), custom_call_target="tpu_custom_call" | custom-call | tf_op jit(solution)/shard_map/pallas_call | solution.py:438
  213.5 1.4 copy.41.weights
  214.9 1.1 compare_convert_fusion.select
  216.0 65.8 %shard_map.139 = bf16[128,2880]{1,0:T(8,128)(2,1)} custom-call(bf16[16,80,2880]{2,1,0:T(8,128)(2,1)} %shard_map.138.partial, bf16[16,128,80]{2,1,0:T(8,128)(2,1)} %compare_convert_fusion.select, f32[16,128,1]{2,1,0:T(8,128)} %copy.41.weights, bf16[128,2880]{1,0:T(8,128)(2,1)} %get-tuple-element.14.mixed), custom_call_target="tpu_custom_call" | custom-call | tf_op jit(solution)/shard_map/pallas_call | solution.py:438
  281.8 2.3 copy.42
  (21 shorter events, 0.1 us)
Async XLA Ops:
  0.0 3.4 %copy-start.1 = (bf16[2880,256]{1,0:T(8,128)(2,1)S(1)}, bf16[2880,256]{1,0:T(8,128)(2,1)}, u32[]{:S(2)}) copy-start(bf16[2880,256]{1,0:T(8,128)(2,1)} %param.18) | copy-start | bytes 4423684
  6.7 1.5 copy-start.4
  6.7 1.6 copy-start.5
  8.2 64.9 %copy-start.6 = (s32[4]{0:T(128)S(1)}, s32[4]{0:T(128)}, u32[]{:S(2)}) copy-start(s32[4]{0:T(128)} %param.15) | copy-start | bytes 52
  8.2 65.9 %copy-start.2 = (bf16[128,2880]{0,1:T(8,128)(2,1)S(1)}, bf16[128,2880]{0,1:T(8,128)(2,1)}, u32[]{:S(2)}) copy-start(bf16[128,2880]{0,1:T(8,128)(2,1)} %param.21) | copy-start | bytes 2211844
  71.6 3.7 %copy-start = (bf16[128,2880]{0,1:T(8,128)(2,1)S(1)}, bf16[128,2880]{0,1:T(8,128)(2,1)}, u32[]{:S(2)}) copy-start(bf16[128,2880]{0,1:T(8,128)(2,1)} %param.14) | copy-start | bytes 2211844
  74.1 2.3 copy-start.3
